TPU v7x, 256 devices: a whole 4x4x8 slice. The times are simulated.
256 devices in a mesh: view: 16 (over z, core), blk: 16 (over y, x).
Axes of the slice: x: 4, y: 4, z: 8, core: 2. Of those that a mesh axis runs over, the one named last changes fastest.
Arguments:
- estimate: float32 [256, 128, 128], P('blk'), may hold values from 0.5 to 2
- images: bfloat16 [16, 256, 64, 128], P('view', 'blk'), may hold values from 0.5 to 2
- point_spread: float32 [8, 9, 7, 25], replicated, may hold values from 0.01 to 1
- covered: int32 [8, 16, 4], P(None, 'blk'), may hold values from 0 to 1, as said below
Outputs:
- estimate_next: float32 [256, 128, 128], P('blk')
Inputs may be any that keep to these rules, and one draw needn't show every extreme that they name: For each view and each block layer along the first dimension, the covered blocks are consecutive along the second dimension and at most 3; for every view some block layer has exactly 3.
All inputs are finite; a program needn't handle non-finite values.
Results may differ from a plain program's by a relative error of at most 0.0003.
Values may be sent and summed in bfloat16 or wider, within the bound.
A program may use at most 64 MiB of HBM per device.

v0:
```python
import jax
import jax.numpy as jnp
from jax import lax
from jax.sharding import PartitionSpec as P

BY = 32


def with_halo(cells, sides, width):
    for axis, dim in sides:
        count = lax.axis_size(axis)
        ends = count - 1
        head = lax.slice_in_dim(cells, 0, width, axis=dim)
        tail = lax.slice_in_dim(cells, cells.shape[dim] - width, cells.shape[dim], axis=dim)
        cells = jnp.concatenate(
            [
                lax.ppermute(tail, axis, [(i, (i + 1) % count) for i in range(ends)]),
                cells,
                lax.ppermute(head, axis, [((i + 1) % count, i) for i in range(ends)]),
            ],
            axis=dim,
        )
    return cells


def swapped(block, axis, stride):
    count = lax.axis_size(axis)
    route = []
    for low in range(count):
        high = low | 1 << stride
        if high != low and high < count:
            route += [(low, high), (high, low)]
    return lax.ppermute(block, axis, route)


def merged(part, axis, combine):
    gathered = lax.all_gather(part, axis)

    def take(source):
        return lax.dynamic_index_in_dim(gathered, source, 0, False)

    return lax.fori_loop(
        1, lax.axis_size(axis), lambda source, state: combine(state, take(source)), take(0)
    )


def band_table(kernel, depth):
    taps_x, taps_y, taps_z = kernel.shape
    span_z = depth + taps_z - 1
    shape_three = (taps_z, span_z, depth)
    offset = lax.broadcasted_iota(jnp.int32, shape_three, 1) - lax.broadcasted_iota(
        jnp.int32, shape_three, 2
    )
    onehot = (offset == lax.broadcasted_iota(jnp.int32, shape_three, 0)).astype(jnp.bfloat16)
    banded = jnp.einsum("abt,tpz->abpz", kernel, onehot, preferred_element_type=jnp.float32).astype(
        jnp.bfloat16
    )
    inner_width = taps_y * span_z
    padded_width = -(-inner_width // 128) * 128
    banded = banded.reshape(taps_x, inner_width, depth)
    return jnp.pad(banded, ((0, 0), (0, padded_width - inner_width), (0, 0)))


def convolve(padded_part, banded, rows_x, rows_y):
    taps_x = padded_part.shape[0] - rows_x + 1
    taps_y = padded_part.shape[1] - rows_y + 1
    columns = jnp.concatenate(
        [padded_part[:, step_y : step_y + rows_y, :] for step_y in range(taps_y)], axis=2
    )
    columns = jnp.pad(columns, ((0, 0), (0, 0), (0, banded.shape[1] - columns.shape[2])))
    output = None
    for shift_x in range(taps_x):
        partial_sum = jnp.dot(
            columns[shift_x : shift_x + rows_x].reshape(rows_x * rows_y, -1),
            banded[shift_x],
            preferred_element_type=jnp.float32,
        )
        output = partial_sum if output is None else output + partial_sum
    return output.reshape(rows_x, rows_y, -1)


def local(estimate, images, point_spread, covered):
    slab_x, width_y, depth = estimate.shape
    share_w = images.shape[2]
    view_count, taps_x, taps_y, taps_z = point_spread.shape
    rim_x, rim_y, rim_z = ((taps_x - 1) // 2, (taps_y - 1) // 2, (taps_z - 1) // 2)
    shares = width_y // share_w
    share_blocks = share_w // BY
    group = lax.axis_index("view")
    view_id = group // shares
    part = group % shares
    y_start = part * share_w
    source = estimate.astype(jnp.bfloat16)
    rimmed = with_halo(source, (("blk", 0),), rim_x)
    padded = jnp.pad(rimmed, ((0, 0), (rim_y, rim_y), (rim_z, rim_z)))
    spread = lax.dynamic_index_in_dim(point_spread, view_id, 0, keepdims=False)
    kernel = (spread / jnp.sum(spread)).astype(jnp.bfloat16)
    forward = band_table(kernel, depth)
    backward = band_table(kernel[::-1, ::-1, ::-1], depth)
    coverage_row = lax.dynamic_index_in_dim(covered[:, 0, :], view_id, 0, keepdims=False) > 0
    share_cover = lax.dynamic_slice_in_dim(coverage_row, part * share_blocks, share_blocks)
    cell_cover = jnp.repeat(share_cover, BY)[None, :, None]
    image = images[0]
    region = lax.dynamic_slice(
        padded, (0, y_start, 0), (slab_x + 2 * rim_x, share_w + 2 * rim_y, depth + 2 * rim_z)
    )
    blurred = convolve(region, forward, slab_x, share_w)
    quotient = jnp.where(cell_cover, image.astype(jnp.float32) / blurred, 0.0).astype(jnp.bfloat16)
    rim_zeros = jnp.zeros((slab_x, rim_y, depth), jnp.bfloat16)
    edge_rows = jnp.where(part == 0, quotient[:, share_w - rim_y :, :], quotient[:, :rim_y, :])
    partner = swapped(edge_rows, "view", 0)
    lower_rim = jnp.where(part > 0, partner, rim_zeros)
    upper_rim = jnp.where(part < shares - 1, partner, rim_zeros)
    extended = jnp.concatenate([lower_rim, quotient, upper_rim], axis=1)
    quotient_rimmed = with_halo(extended, (("blk", 0),), rim_x)
    padded_quotient = jnp.pad(quotient_rimmed, ((0, 0), (0, 0), (rim_z, rim_z)))
    correction = convolve(padded_quotient, backward, slab_x, share_w)
    share_factor = jnp.where(cell_cover, correction, 1.0)
    n_view = lax.axis_size("view")
    step_x = slab_x // n_view
    rows = share_factor.reshape(n_view, step_x, share_w, depth)
    got = lax.all_to_all(rows, "view", 0, 0)
    got = got.reshape(n_view // shares, shares, step_x, share_w, depth)
    product_rows = jnp.prod(got, axis=0)
    product_rows = jnp.transpose(product_rows, (1, 0, 2, 3)).reshape(step_x, width_y, depth)
    mine = lax.dynamic_slice_in_dim(estimate, group * step_x, step_x, axis=0)
    return lax.all_gather(mine * product_rows, "view", axis=0, tiled=True)


def solution(mesh):
    in_specs = (P("blk", None, None), P("view", "blk", None, None), P(), P(None, "blk", None))
    out_specs = P("blk", None, None)
    return jax.shard_map(local, mesh=mesh, in_specs=in_specs, out_specs=out_specs, check_vma=False)
```

profile of v0, /device:TPU:1, one launch (start us, length us, event | category | flops | bytes accessed | tf_op | source)
XLA Modules:
  0.0 175.8 jit_solution(12433264027804252495)
XLA Ops:
  6.5 1.3 convert_element_type.38
  7.9 4.0 %collective-permute-start = (bf16[4,128,128]{2,1,0:T(8,128)(2,1)S(1)}, bf16[4,128,128]{2,1,0:T(8,128)(2,1)S(1)}, u32[]{:S(2)}, u32[]{:S(2)}) collective-permute-start(bf16[4,128,128]{2,1,0:T(8,128)(2,1)S(1)} %get-tuple-element.40), channel_id=1, source_target_pairs={{0,1},{1,2},{2,3},{3,4},{4,5},{5,6},{6,7},{7,8},{8,9},{9,10},{10,1... | collective-permute-start | bytes 393224 | tf_op jit(solution)/shard_map/ppermute | solution.py:17
  11.8 1.3 collective-permute-start.1
  13.2 1.7 fusion.97
  14.8 3.2 %fusion.10 = bf16[9,7,152,128]{3,1,2,0:T(8,128)(2,1)} fusion(f32[1,9,7,25]{3,0,2,1:T(1,128)S(1)} %get-tuple-element.6, f32[]{:T(128)} %get-tuple-element.5), kind=kOutput, calls=%fused_computation.13 | convolution fusion | flops 63488080 | bytes 2457760 | tf_op jit(solution)/shard_map/abt,tpz->abpz/dot_general | solution.py:55
  18.0 1.6 iota_compare_fusion
  19.6 2.1 %copy.10 = bf16[9,7,152,128]{3,2,1,0:T(8,128)(2,1)S(1)} copy(bf16[9,7,152,128]{3,1,2,0:T(8,128)(2,1)} %fusion.10) | data formatting | bytes 4902912 | tf_op jit(solution)/shard_map/convert_element_type | solution.py:55
  22.1 2.9 %fusion.23 = bf16[24,70,152]{2,1,0:T(8,128)(2,1)S(1)} fusion(s32[]{:T(128)S(6)} %select_n.67, bf16[4,128,128]{2,1,0:T(8,128)(2,1)S(1)} %collective-permute-done, bf16[16,128,128]{2,1,0:T(8,128)(2,1)S(1)} %convert_element_type.38, pred[24,134,152]{2,1,0:T(8,128)(4,1)} %get-tuple-element.45, pred[24,134,152]{2,1,0:T(8,128)(4,1)} %get-tuple-element.46, ...), kind=kLoop, calls=%fused_computation.61 | loop fusion | flops 5873280 | bytes 1808896 | tf_op jit(solution)/shard_map/concatenate | solution.py:15
  25.0 3.1 %fusion.99 = (bf16[24,64,152]{2,1,0:T(8,128)(2,1)S(1)}, bf16[24,64,152]{2,1,0:T(8,128)(2,1)}, bf16[24,64,152]{2,1,0:T(8,128)(2,1)}, bf16[24,64,152]{2,1,0:T(8,12...) fusion(bf16[24,70,152]{2,1,0:T(8,128)(2,1)S(1)} %fusion.23), kind=kLoop, calls=%fused_computation.152 | loop fusion | bytes 6537216 | tf_op jit(solution)/shard_map/slice | solution.py:68
  28.1 8.4 %concatenate.16 = bf16[24,64,1064]{2,1,0:T(8,128)(2,1)} concatenate(bf16[24,64,152]{2,1,0:T(8,128)(2,1)} %get-tuple-element.38, bf16[24,64,152]{2,1,0:T(8,128)(2,1)} %get-tuple-element.37, bf16[24,64,152]{2,1,0:T(8,128)(2,1)} %get-tuple-element.36, bf16[24,64,152]{2,1,0:T(8,128)(2,1)} %get-tuple-element.35, bf16[24,64,152]{2,1,0:T(8,128)(2,1)} %get-tuple-element.34, ...), dimensions={2} | concatenate | bytes 6537216 | tf_op jit(solution)/shard_map/concatenate | solution.py:67
  36.5 12.6 %pad_slice_fusion.27 = (bf16[16,64,1152]{2,1,0:T(8,128)(2,1)S(1)}, bf16[16,64,1152]{2,1,0:T(8,128)(2,1)S(1)}, bf16[16,64,1152]{2,1,0:T(8,128)(2,1)S(1)}, bf16[16...) fusion(bf16[24,64,1064]{2,1,0:T(8,128)(2,1)} %concatenate.16), kind=kLoop, calls=%fused_computation.106 | loop fusion | bytes 24502272 | tf_op jit(solution)/shard_map/slice | solution.py:74
  51.5 0.8 convolution_add_fusion.13
  52.3 0.8 convolution_add_fusion.12
  53.1 0.8 convolution_add_fusion.11
  54.6 0.8 convolution_add_fusion.9
  56.6 1.1 collective-permute-start.2
  58.6 1.3 collective-permute-start.4
  59.9 4.9 %collective-permute-start.3 = (bf16[4,70,128]{2,1,0:T(8,128)(2,1)S(1)}, bf16[4,70,128]{2,1,0:T(8,128)(2,1)S(1)}, u32[]{:S(2)}, u32[]{:S(2)}) collective-permute-start(bf16[4,70,128]{2,1,0:T(8,128)(2,1)S(1)} %get-tuple-element.41), channel_id=1, source_target_pairs={{0,1},{1,2},{2,3},{3,4},{4,5},{5,6},{6,7},{7,8},{8,9},{9,10},{10,1... | collective-permute-start | bytes 215048 | tf_op jit(solution)/shard_map/ppermute | solution.py:17
  64.8 1.0 fusion.13
  66.8 3.1 %fusion.98 = (bf16[24,64,152]{2,1,0:T(8,128)(2,1)S(1)}, bf16[24,64,152]{2,1,0:T(8,128)(2,1)}, bf16[24,64,152]{2,1,0:T(8,128)(2,1)}, bf16[24,64,152]{2,1,0:T(8,12...) fusion(bf16[24,70,152]{2,1,0:T(8,128)(2,1)S(1)} %select_maximum_fusion), kind=kLoop, calls=%fused_computation.151 | loop fusion | bytes 6537216 | tf_op jit(solution)/shard_map/slice | solution.py:68
  70.0 8.4 %concatenate.19 = bf16[24,64,1064]{2,1,0:T(8,128)(2,1)} concatenate(bf16[24,64,152]{2,1,0:T(8,128)(2,1)} %get-tuple-element.31, bf16[24,64,152]{2,1,0:T(8,128)(2,1)} %get-tuple-element.30, bf16[24,64,152]{2,1,0:T(8,128)(2,1)} %get-tuple-element.29, bf16[24,64,152]{2,1,0:T(8,128)(2,1)} %get-tuple-element.28, bf16[24,64,152]{2,1,0:T(8,128)(2,1)} %get-tuple-element.27, ...), dimensions={2} | concatenate | bytes 6537216 | tf_op jit(solution)/shard_map/concatenate | solution.py:67
  78.4 12.6 %pad_slice_fusion.18 = (bf16[16,64,1152]{2,1,0:T(8,128)(2,1)S(1)}, bf16[16,64,1152]{2,1,0:T(8,128)(2,1)S(1)}, bf16[16,64,1152]{2,1,0:T(8,128)(2,1)S(1)}, bf16[16...) fusion(bf16[24,64,1064]{2,1,0:T(8,128)(2,1)} %concatenate.19), kind=kLoop, calls=%fused_computation.97 | loop fusion | bytes 24502272 | tf_op jit(solution)/shard_map/slice | solution.py:74
  91.8 0.8 convolution_add_fusion.7
  92.6 0.8 convolution_add_fusion.6
  94.9 0.8 convolution_add_fusion.3
  97.3 0.8 convolution_add_fusion
  98.1 0.9 broadcast_select_fusion
  99.0 9.7 %all-to-all-start = ((f32[16,1,64,128]{3,2,1,0:T(8,128)}), f32[16,1,64,128]{3,2,1,0:T(8,128)S(1)}, u32[]{:S(2)}, u32[]{:S(2)}) async-start(f32[16,1,64,128]{3,2,1,0:T(8,128)} %broadcast_select_fusion), calls=%async_computation | async-start | bytes 1048576 | tf_op jit(solution)/shard_map/all_to_all | solution.py:122
  108.7 17.3 %all-to-all-done = f32[16,1,64,128]{3,2,1,0:T(8,128)S(1)} async-done(((f32[16,1,64,128]{3,2,1,0:T(8,128)}), f32[16,1,64,128]{3,2,1,0:T(8,128)S(1)}, u32[]{:S(2)}, u32[]{:S(2)}) %all-to-all-start) | async-done | bytes 524320 | tf_op jit(solution)/shard_map/all_to_all | solution.py:122
  126.0 1.5 bitcast_multiply_fusion
  127.5 39.1 %all-gather.2.cloned.1.call-done = f32[16,128,128]{2,1,0:T(8,128)} async-done(((f32[1,128,128]{2,1,0:T(8,128)}), f32[16,128,128]{2,1,0:T(8,128)}) %all-gather.2.cloned.1.call-update) | async-done | bytes 1048592 | tf_op jit(solution)/shard_map/all_gather | solution.py:127
  166.7 2.3 %copy.26 = f32[16,128,128]{2,1,0:T(8,128)} copy(f32[16,128,128]{2,1,0:T(8,128)} %all-gather.2.cloned.1.call-done) | data formatting | bytes 2097152
  (35 shorter events, 10.6 us)
Async XLA Ops:
  7.9 14.2 %collective-permute-start = (bf16[4,128,128]{2,1,0:T(8,128)(2,1)S(1)}, bf16[4,128,128]{2,1,0:T(8,128)(2,1)S(1)}, u32[]{:S(2)}, u32[]{:S(2)}) collective-permute-start(bf16[4,128,128]{2,1,0:T(8,128)(2,1)S(1)} %get-tuple-element.40), channel_id=1, source_target_pairs={{0,1},{1,2},{2,3},{3,4},{4,5},{5,6},{6,7},{7,8},{8,9},{9,10},{10,1... | collective-permute-start | bytes 393224 | tf_op jit(solution)/shard_map/ppermute | solution.py:17
  11.8 10.3 %collective-permute-start.1 = (bf16[4,128,128]{2,1,0:T(8,128)(2,1)S(1)}, bf16[4,128,128]{2,1,0:T(8,128)(2,1)S(1)}, u32[]{:S(2)}, u32[]{:S(2)}) collective-permute-start(bf16[4,128,128]{2,1,0:T(8,128)(2,1)S(1)} %get-tuple-element.39), channel_id=1, source_target_pairs={{1,0},{2,1},{3,2},{4,3},{5,4},{6,5},{7,6},{8,7},{9,8},{10,9},{11,1... | collective-permute-start | bytes 393224 | tf_op jit(solution)/shard_map/ppermute | solution.py:19
  19.6 2.2 %copy-start.1 = (s32[8,1,4]{0,2,1:T(4,128)S(1)}, s32[8,1,4]{0,2,1:T(4,128)}, u32[]{:S(2)}) copy-start(s32[8,1,4]{0,2,1:T(4,128)} %param.7) | copy-start | bytes 388
  55.4 1.0 copy-start
  56.6 1.9 %collective-permute-start.2 = (bf16[16,3,128]{2,1,0:T(4,128)(2,1)S(1)}, bf16[16,3,128]{2,1,0:T(4,128)(2,1)S(1)}, u32[]{:S(2)}, u32[]{:S(2)}) collective-permute-start(bf16[16,3,128]{2,1,0:T(4,128)(2,1)S(1)} %slice_select_fusion), channel_id=1, source_target_pairs={{0,16},{16,0},{32,48},{48,32},{64,80},{80,64},{96,112},{112,96},{1... | collective-permute-start | bytes 36872 | tf_op jit(solution)/shard_map/ppermute | solution.py:33
  58.6 7.5 %collective-permute-start.4 = (bf16[4,70,128]{2,1,0:T(8,128)(2,1)S(1)}, bf16[4,70,128]{2,1,0:T(8,128)(2,1)S(1)}, u32[]{:S(2)}, u32[]{:S(2)}) collective-permute-start(bf16[4,70,128]{2,1,0:T(8,128)(2,1)S(1)} %get-tuple-element.42), channel_id=1, source_target_pairs={{1,0},{2,1},{3,2},{4,3},{5,4},{6,5},{7,6},{8,7},{9,8},{10,9},{11,1... | collective-permute-start | bytes 215048 | tf_op jit(solution)/shard_map/ppermute | solution.py:19
  59.9 6.3 %collective-permute-start.3 = (bf16[4,70,128]{2,1,0:T(8,128)(2,1)S(1)}, bf16[4,70,128]{2,1,0:T(8,128)(2,1)S(1)}, u32[]{:S(2)}, u32[]{:S(2)}) collective-permute-start(bf16[4,70,128]{2,1,0:T(8,128)(2,1)S(1)} %get-tuple-element.41), channel_id=1, source_target_pairs={{0,1},{1,2},{2,3},{3,4},{4,5},{5,6},{6,7},{7,8},{8,9},{9,10},{10,1... | collective-permute-start | bytes 215048 | tf_op jit(solution)/shard_map/ppermute | solution.py:17
  99.0 27.0 %all-to-all-start = ((f32[16,1,64,128]{3,2,1,0:T(8,128)}), f32[16,1,64,128]{3,2,1,0:T(8,128)S(1)}, u32[]{:S(2)}, u32[]{:S(2)}) async-start(f32[16,1,64,128]{3,2,1,0:T(8,128)} %broadcast_select_fusion), calls=%async_computation | async-start | bytes 1048576 | tf_op jit(solution)/shard_map/all_to_all | solution.py:122
  108.7 58.0 %all-gather.2.cloned.1.call-start = ((), (), s32[]{:S(2)}) async-start(), calls=%async_computation.1 | async-start | bytes 1114112 | tf_op jit(solution)/shard_map/all_gather | solution.py:127
Sparse Core Ops, SparseCore 0:
  127.7 38.9 all-gather.1
where the time goes:
time: 177 us; the launch traced here: 176 us
  waiting for transfers between devices  56.6 us (32%)
  local copies, waits for them, and re-layouts  53.6 us (30%)
  starting transfers between devices  22.2 us (13%)
  matrix products  18.2 us (10%)
  between operations  13.7 us (8%)
  other arithmetic  11.5 us (6%)
    all_gather x1, waiting for transfers between devices, local(): return lax.all_gather(mine * product_rows, 'view', axis=0, tiled=True)  39.1 us
    slice x2, local copies, waits for them, and re-layouts, convolve(): columns[shift_x:shift_x + rows_x].reshape(rows_x * rows_y, -1)  25.2 us
    all_to_all x1, waiting for transfers between devices, local(): got = lax.all_to_all(rows, 'view', 0, 0)  17.3 us
    concatenate x2, local copies, waits for them, and re-layouts, convolve(): jnp.concatenate([padded_part[:, step_y:step_y + rows_y, :] for step_y in...  16.9 us
    dot_general x18, matrix products, convolve(): jnp.dot(columns[shift_x:shift_x + rows_x].reshape(rows_x * rows_y, -1), b...  14 us
    all_to_all x1, starting transfers between devices, local(): got = lax.all_to_all(rows, 'view', 0, 0)  9.68 us
    ppermute x2, starting transfers between devices, with_halo(): lax.ppermute(tail, axis, [(i, (i + 1) % count) for i in range(ends)])  8.85 us
    slice x2, local copies, waits for them, and re-layouts, convolve(): padded_part[:, step_y:step_y + rows_y, :]  6.25 us
  transfers between devices with their start and end apart: 7, of which 4 were waited for; matrix products, arithmetic and copies ran while one was open for 6% of the time, Pallas kernels for 0%

commit v1 on v0

--- a/solution.py
+++ b/solution.py
@@ -124,7 +124,10 @@
     product_rows = jnp.prod(got, axis=0)
     product_rows = jnp.transpose(product_rows, (1, 0, 2, 3)).reshape(step_x, width_y, depth)
     mine = lax.dynamic_slice_in_dim(estimate, group * step_x, step_x, axis=0)
-    return lax.all_gather(mine * product_rows, "view", axis=0, tiled=True)
+    return jnp.concatenate(
+        lax.all_to_all(jnp.stack([mine * product_rows] * lax.axis_size("view")), "view", 0, 0),
+        axis=0,
+    )
 
 
 def solution(mesh):

time: 177 us -> 158 us (0.89)
  the two profiles are of different devices: /device:TPU:1 before, /device:TPU:25 now
where the time goes in v1:
time: 158 us; the launch traced here: 157 us
  local copies, waits for them, and re-layouts  51.4 us (33%)
  blocking collectives  31.3 us (20%)
  starting transfers between devices  24.3 us (15%)
  waiting for transfers between devices  20.4 us (13%)
  matrix products  18.2 us (12%)
  other arithmetic  10.9 us (7%)
    all_to_all x1, blocking collectives, local(): lax.all_to_all(jnp.stack([mine * product_rows] * lax.axis_size('view')),...  31.3 us
    slice x2, local copies, waits for them, and re-layouts, convolve(): columns[shift_x:shift_x + rows_x].reshape(rows_x * rows_y, -1)  24.2 us
    all_to_all x1, waiting for transfers between devices, local(): got = lax.all_to_all(rows, 'view', 0, 0)  17.3 us
    concatenate x2, local copies, waits for them, and re-layouts, convolve(): jnp.concatenate([padded_part[:, step_y:step_y + rows_y, :] for step_y in...  16.9 us
    dot_general x18, matrix products, convolve(): jnp.dot(columns[shift_x:shift_x + rows_x].reshape(rows_x * rows_y, -1), b...  14 us
    all_to_all x1, starting transfers between devices, local(): got = lax.all_to_all(rows, 'view', 0, 0)  10.3 us
    ppermute x2, starting transfers between devices, with_halo(): lax.ppermute(head, axis, [((i + 1) % count, i) for i in range(ends)])  6.73 us
    slice x2, local copies, waits for them, and re-layouts, convolve(): padded_part[:, step_y:step_y + rows_y, :]  6.24 us
  transfers between devices with their start and end apart: 6, of which 3 were waited for; matrix products, arithmetic and copies ran while one was open for 7% of the time, Pallas kernels for 0%

profile of v1, /device:TPU:25, one launch (start us, length us, event | category | flops | bytes accessed | tf_op | source)
XLA Modules:
  0.0 156.8 jit_solution(3442602763010382013)
XLA Ops:
  0.0 1.3 convert_element_type.38
  1.3 3.1 %collective-permute-start = (bf16[4,128,128]{2,1,0:T(8,128)(2,1)S(1)}, bf16[4,128,128]{2,1,0:T(8,128)(2,1)S(1)}, u32[]{:S(2)}, u32[]{:S(2)}) collective-permute-start(bf16[4,128,128]{2,1,0:T(8,128)(2,1)S(1)} %get-tuple-element.40), channel_id=1, source_target_pairs={{0,1},{1,2},{2,3},{3,4},{4,5},{5,6},{6,7},{7,8},{8,9},{9,10},{10,1... | collective-permute-start | bytes 393224 | tf_op jit(solution)/shard_map/ppermute | solution.py:17
  4.5 4.3 %collective-permute-start.1 = (bf16[4,128,128]{2,1,0:T(8,128)(2,1)S(1)}, bf16[4,128,128]{2,1,0:T(8,128)(2,1)S(1)}, u32[]{:S(2)}, u32[]{:S(2)}) collective-permute-start(bf16[4,128,128]{2,1,0:T(8,128)(2,1)S(1)} %get-tuple-element.39), channel_id=1, source_target_pairs={{1,0},{2,1},{3,2},{4,3},{5,4},{6,5},{7,6},{8,7},{9,8},{10,9},{11,1... | collective-permute-start | bytes 393224 | tf_op jit(solution)/shard_map/ppermute | solution.py:19
  8.8 1.7 %fusion.98 = (f32[]{:T(128)}, f32[1,9,7,25]{3,0,2,1:T(1,128)S(1)}) fusion(f32[8,9,7,25]{3,0,2,1:T(8,128)} %param.6, s32[]{:T(128)S(6)} %select_n.62), kind=kLoop, calls=%fused_computation.151 | loop fusion | flops 1574 | bytes 12608 | tf_op jit(solution)/shard_map/reduce_sum | solution.py:97
  10.4 3.2 %fusion.10 = bf16[9,7,152,128]{3,1,2,0:T(8,128)(2,1)} fusion(f32[1,9,7,25]{3,0,2,1:T(1,128)S(1)} %get-tuple-element.6, f32[]{:T(128)} %get-tuple-element.5), kind=kOutput, calls=%fused_computation.13 | convolution fusion | flops 63488080 | bytes 2457760 | tf_op jit(solution)/shard_map/abt,tpz->abpz/dot_general | solution.py:55
  13.6 1.6 %iota_compare_fusion = (pred[24,134,152]{2,1,0:T(8,128)(4,1)}, pred[24,134,152]{2,1,0:T(8,128)(4,1)}) fusion(), kind=kLoop, calls=%fused_computation | loop fusion | flops 977664 | bytes 977664 | tf_op jit(solution)/shard_map/jit(_pad)/pad | solution.py:95
  15.2 2.1 %copy.10 = bf16[9,7,152,128]{3,2,1,0:T(8,128)(2,1)S(1)} copy(bf16[9,7,152,128]{3,1,2,0:T(8,128)(2,1)} %fusion.10) | data formatting | bytes 4902912 | tf_op jit(solution)/shard_map/convert_element_type | solution.py:55
  17.7 2.9 %fusion.23 = bf16[24,70,152]{2,1,0:T(8,128)(2,1)S(1)} fusion(s32[]{:T(128)S(6)} %select_n.67, bf16[4,128,128]{2,1,0:T(8,128)(2,1)S(1)} %collective-permute-done, bf16[16,128,128]{2,1,0:T(8,128)(2,1)S(1)} %convert_element_type.38, pred[24,134,152]{2,1,0:T(8,128)(4,1)} %get-tuple-element.45, pred[24,134,152]{2,1,0:T(8,128)(4,1)} %get-tuple-element.46, ...), kind=kLoop, calls=%fused_computation.61 | loop fusion | flops 5873280 | bytes 1808896 | tf_op jit(solution)/shard_map/concatenate | solution.py:15
  20.6 3.1 %fusion.100 = (bf16[24,64,152]{2,1,0:T(8,128)(2,1)S(1)}, bf16[24,64,152]{2,1,0:T(8,128)(2,1)}, bf16[24,64,152]{2,1,0:T(8,128)(2,1)}, bf16[24,64,152]{2,1,0:T(8,1...) fusion(bf16[24,70,152]{2,1,0:T(8,128)(2,1)S(1)} %fusion.23), kind=kLoop, calls=%fused_computation.153 | loop fusion | bytes 6537216 | tf_op jit(solution)/shard_map/slice | solution.py:68
  23.7 8.4 %concatenate.16 = bf16[24,64,1064]{2,1,0:T(8,128)(2,1)} concatenate(bf16[24,64,152]{2,1,0:T(8,128)(2,1)} %get-tuple-element.38, bf16[24,64,152]{2,1,0:T(8,128)(2,1)} %get-tuple-element.37, bf16[24,64,152]{2,1,0:T(8,128)(2,1)} %get-tuple-element.36, bf16[24,64,152]{2,1,0:T(8,128)(2,1)} %get-tuple-element.35, bf16[24,64,152]{2,1,0:T(8,128)(2,1)} %get-tuple-element.34, ...), dimensions={2} | concatenate | bytes 6537216 | tf_op jit(solution)/shard_map/concatenate | solution.py:67
  32.2 12.1 %pad_slice_fusion.27 = (bf16[16,64,1152]{2,1,0:T(8,128)(2,1)S(1)}, bf16[16,64,1152]{2,1,0:T(8,128)(2,1)S(1)}, bf16[16,64,1152]{2,1,0:T(8,128)(2,1)S(1)}, bf16[16...) fusion(bf16[24,64,1064]{2,1,0:T(8,128)(2,1)} %concatenate.16), kind=kLoop, calls=%fused_computation.106 | loop fusion | bytes 24502272 | tf_op jit(solution)/shard_map/slice | solution.py:74
  45.1 0.8 convolution_add_fusion.15
  46.6 0.8 convolution_add_fusion.13
  49.0 0.8 convolution_add_fusion.10
  49.8 0.8 convolution_add_fusion.9
  50.6 0.8 convolution_add_fusion.8
  51.7 1.4 collective-permute-start.2
  54.0 2.5 %collective-permute-start.4 = (bf16[4,70,128]{2,1,0:T(8,128)(2,1)S(1)}, bf16[4,70,128]{2,1,0:T(8,128)(2,1)S(1)}, u32[]{:S(2)}, u32[]{:S(2)}) collective-permute-start(bf16[4,70,128]{2,1,0:T(8,128)(2,1)S(1)} %get-tuple-element.42), channel_id=1, source_target_pairs={{1,0},{2,1},{3,2},{4,3},{5,4},{6,5},{7,6},{8,7},{9,8},{10,9},{11,1... | collective-permute-start | bytes 215048 | tf_op jit(solution)/shard_map/ppermute | solution.py:19
  56.4 2.8 %collective-permute-start.3 = (bf16[4,70,128]{2,1,0:T(8,128)(2,1)S(1)}, bf16[4,70,128]{2,1,0:T(8,128)(2,1)S(1)}, u32[]{:S(2)}, u32[]{:S(2)}) collective-permute-start(bf16[4,70,128]{2,1,0:T(8,128)(2,1)S(1)} %get-tuple-element.41), channel_id=1, source_target_pairs={{0,1},{1,2},{2,3},{3,4},{4,5},{5,6},{6,7},{7,8},{8,9},{9,10},{10,1... | collective-permute-start | bytes 215048 | tf_op jit(solution)/shard_map/ppermute | solution.py:17
  59.3 1.0 fusion.13
  60.6 3.0 %collective-permute-done.3 = bf16[4,70,128]{2,1,0:T(8,128)(2,1)S(1)} collective-permute-done((bf16[4,70,128]{2,1,0:T(8,128)(2,1)S(1)}, bf16[4,70,128]{2,1,0:T(8,128)(2,1)S(1)}, u32[]{:S(2)}, u32[]{:S(2)}) %collective-permute-start.3) | collective-permute-done | bytes 71712 | tf_op jit(solution)/shard_map/ppermute | solution.py:17
  64.3 3.1 %fusion.99 = (bf16[24,64,152]{2,1,0:T(8,128)(2,1)S(1)}, bf16[24,64,152]{2,1,0:T(8,128)(2,1)}, bf16[24,64,152]{2,1,0:T(8,128)(2,1)}, bf16[24,64,152]{2,1,0:T(8,12...) fusion(bf16[24,70,152]{2,1,0:T(8,128)(2,1)S(1)} %select_maximum_fusion), kind=kLoop, calls=%fused_computation.152 | loop fusion | bytes 6537216 | tf_op jit(solution)/shard_map/slice | solution.py:68
  67.5 8.5 %concatenate.19 = bf16[24,64,1064]{2,1,0:T(8,128)(2,1)} concatenate(bf16[24,64,152]{2,1,0:T(8,128)(2,1)} %get-tuple-element.31, bf16[24,64,152]{2,1,0:T(8,128)(2,1)} %get-tuple-element.30, bf16[24,64,152]{2,1,0:T(8,128)(2,1)} %get-tuple-element.29, bf16[24,64,152]{2,1,0:T(8,128)(2,1)} %get-tuple-element.28, bf16[24,64,152]{2,1,0:T(8,128)(2,1)} %get-tuple-element.27, ...), dimensions={2} | concatenate | bytes 6537216 | tf_op jit(solution)/shard_map/concatenate | solution.py:67
  75.9 12.1 %pad_slice_fusion.18 = (bf16[16,64,1152]{2,1,0:T(8,128)(2,1)S(1)}, bf16[16,64,1152]{2,1,0:T(8,128)(2,1)S(1)}, bf16[16,64,1152]{2,1,0:T(8,128)(2,1)S(1)}, bf16[16...) fusion(bf16[24,64,1064]{2,1,0:T(8,128)(2,1)} %concatenate.19), kind=kLoop, calls=%fused_computation.97 | loop fusion | bytes 24502272 | tf_op jit(solution)/shard_map/slice | solution.py:74
  89.6 0.8 convolution_add_fusion.6
  91.2 0.8 convolution_add_fusion.4
  95.1 0.9 broadcast_select_fusion
  96.0 10.3 %all-to-all-start = ((f32[16,1,64,128]{3,2,1,0:T(8,128)}), f32[16,1,64,128]{3,2,1,0:T(8,128)S(1)}, u32[]{:S(2)}, u32[]{:S(2)}) async-start(f32[16,1,64,128]{3,2,1,0:T(8,128)} %broadcast_select_fusion), calls=%async_computation | async-start | bytes 1048576 | tf_op jit(solution)/shard_map/all_to_all | solution.py:122
  106.3 17.3 %all-to-all-done = f32[16,1,64,128]{3,2,1,0:T(8,128)S(1)} async-done(((f32[16,1,64,128]{3,2,1,0:T(8,128)}), f32[16,1,64,128]{3,2,1,0:T(8,128)S(1)}, u32[]{:S(2)}, u32[]{:S(2)}) %all-to-all-start) | async-done | bytes 524320 | tf_op jit(solution)/shard_map/all_to_all | solution.py:122
  123.6 0.9 fusion.72
  124.6 31.3 %all_to_all.10 = f32[16,1,128,128]{3,2,1,0:T(8,128)S(1)} all-to-all(f32[16,1,128,128]{3,2,1,0:T(8,128)S(1)} %stack.2), channel_id=1, replica_groups=mesh['view'=16,'blk'=16] {'view'}, dimensions={0} | all-to-all | bytes 2097152 | tf_op jit(solution)/shard_map/all_to_all | solution.py:128
  155.8 1.0 copy.26
  (34 shorter events, 11.3 us)
Async XLA Ops:
  1.3 16.4 %collective-permute-start = (bf16[4,128,128]{2,1,0:T(8,128)(2,1)S(1)}, bf16[4,128,128]{2,1,0:T(8,128)(2,1)S(1)}, u32[]{:S(2)}, u32[]{:S(2)}) collective-permute-start(bf16[4,128,128]{2,1,0:T(8,128)(2,1)S(1)} %get-tuple-element.40), channel_id=1, source_target_pairs={{0,1},{1,2},{2,3},{3,4},{4,5},{5,6},{6,7},{7,8},{8,9},{9,10},{10,1... | collective-permute-start | bytes 393224 | tf_op jit(solution)/shard_map/ppermute | solution.py:17
  4.5 13.2 %collective-permute-start.1 = (bf16[4,128,128]{2,1,0:T(8,128)(2,1)S(1)}, bf16[4,128,128]{2,1,0:T(8,128)(2,1)S(1)}, u32[]{:S(2)}, u32[]{:S(2)}) collective-permute-start(bf16[4,128,128]{2,1,0:T(8,128)(2,1)S(1)} %get-tuple-element.39), channel_id=1, source_target_pairs={{1,0},{2,1},{3,2},{4,3},{5,4},{6,5},{7,6},{8,7},{9,8},{10,9},{11,1... | collective-permute-start | bytes 393224 | tf_op jit(solution)/shard_map/ppermute | solution.py:19
  15.2 2.2 %copy-start.1 = (s32[8,1,4]{0,2,1:T(4,128)S(1)}, s32[8,1,4]{0,2,1:T(4,128)}, u32[]{:S(2)}) copy-start(s32[8,1,4]{0,2,1:T(4,128)} %param.7) | copy-start | bytes 388
  50.6 1.0 copy-start
  51.7 2.2 %collective-permute-start.2 = (bf16[16,3,128]{2,1,0:T(4,128)(2,1)S(1)}, bf16[16,3,128]{2,1,0:T(4,128)(2,1)S(1)}, u32[]{:S(2)}, u32[]{:S(2)}) collective-permute-start(bf16[16,3,128]{2,1,0:T(4,128)(2,1)S(1)} %slice_select_fusion), channel_id=1, source_target_pairs={{0,16},{16,0},{32,48},{48,32},{64,80},{80,64},{96,112},{112,96},{1... | collective-permute-start | bytes 36872 | tf_op jit(solution)/shard_map/ppermute | solution.py:33
  54.0 6.6 %collective-permute-start.4 = (bf16[4,70,128]{2,1,0:T(8,128)(2,1)S(1)}, bf16[4,70,128]{2,1,0:T(8,128)(2,1)S(1)}, u32[]{:S(2)}, u32[]{:S(2)}) collective-permute-start(bf16[4,70,128]{2,1,0:T(8,128)(2,1)S(1)} %get-tuple-element.42), channel_id=1, source_target_pairs={{1,0},{2,1},{3,2},{4,3},{5,4},{6,5},{7,6},{8,7},{9,8},{10,9},{11,1... | collective-permute-start | bytes 215048 | tf_op jit(solution)/shard_map/ppermute | solution.py:19
  56.4 7.2 %collective-permute-start.3 = (bf16[4,70,128]{2,1,0:T(8,128)(2,1)S(1)}, bf16[4,70,128]{2,1,0:T(8,128)(2,1)S(1)}, u32[]{:S(2)}, u32[]{:S(2)}) collective-permute-start(bf16[4,70,128]{2,1,0:T(8,128)(2,1)S(1)} %get-tuple-element.41), channel_id=1, source_target_pairs={{0,1},{1,2},{2,3},{3,4},{4,5},{5,6},{6,7},{7,8},{8,9},{9,10},{10,1... | collective-permute-start | bytes 215048 | tf_op jit(solution)/shard_map/ppermute | solution.py:17
  96.0 27.6 %all-to-all-start = ((f32[16,1,64,128]{3,2,1,0:T(8,128)}), f32[16,1,64,128]{3,2,1,0:T(8,128)S(1)}, u32[]{:S(2)}, u32[]{:S(2)}) async-start(f32[16,1,64,128]{3,2,1,0:T(8,128)} %broadcast_select_fusion), calls=%async_computation | async-start | bytes 1048576 | tf_op jit(solution)/shard_map/all_to_all | solution.py:122
